TPU v7x, 32 devices: a whole 2x2x4 slice. The times are simulated.
32 devices in a mesh: ctx: 8 (over y, x, core), wa: 4 (over z).
Axes of the slice: x: 2, y: 2, z: 4, core: 2. Of those that a mesh axis runs over, the one named last changes fastest.
Arguments:
- tokens: bfloat16 [8, 1024, 768], P('wa', 'ctx'), may hold values from -6 to 6
- doc_lengths: int32 [8], replicated, may hold values from 256 to 1024, as said below
- group_deal: int32 [8, 8], replicated, may hold values from 0 to 7, each once within a row
- qkv_weight: bfloat16 [768, 2304], P('wa'), may hold values from -0.21875 to 0.21875
- out_weight: bfloat16 [768, 768], P('wa'), may hold values from -2.5 to 2.5
- up_weight: bfloat16 [768, 3072], P('wa'), may hold values from -0.21875 to 0.21875
- up_bias: bfloat16 [3072], P('wa'), may hold values from -3 to 3
- down_weight: bfloat16 [3072, 768], P('wa'), may hold values from -0.109375 to 0.109375
- proj_weight: bfloat16 [768, 128], P('wa'), may hold values from -0.21875 to 0.21875
- vectors: bfloat16 [8, 768], P(None, 'wa'), may hold values from -2 to 2
- cotangent: bfloat16 [8, 1024, 128], P('wa', 'ctx'), may hold values from -6 to 6
Outputs:
- embeddings: bfloat16 [8, 1024, 128], P('wa', 'ctx')
- tokens_grad: float32 [8, 1024, 768], P('wa', 'ctx')
- qkv_grad: float32 [768, 2304], P('wa')
- out_grad: float32 [768, 768], P('wa')
- up_grad: float32 [768, 3072], P('wa')
- bias_grad: float32 [3072], P('wa')
- down_grad: float32 [3072, 768], P('wa')
- proj_grad: float32 [768, 128], P('wa')
- vectors_grad: float32 [8, 768], P(None, 'wa')
Inputs may be any that keep to these rules, and one draw needn't show every extreme that they name: `doc_lengths`: every draw has a sequence with all 1024 slots valid. `group_deal`: each row is a permutation of the block numbers of a sequence.
All inputs are finite; a program needn't handle non-finite values.
Results may differ from a plain program's by a relative error of at most 0.023.
Values may be sent and summed in bfloat16 or wider, within the bound.
No kernel may reach another device: no remote copies, remote signals or barrier semaphores. Data moves between devices by JAX's collectives and lax.ppermute only.
A program may use at most 256 MiB of HBM per device.

v0:
```python
from functools import partial
import jax
import jax.numpy as jnp
from jax import lax
from jax.sharding import PartitionSpec as P

H = 12
HEAD = 64
NEG_FILL = -1e30
NORM_EPS = 1e-06
ROOT_HALF = 0.7071067811865476
DENSITY_SCALE = 0.3989422804014327


def norm_rows(inputs, gain_row, shift_row):
    middle = jnp.mean(inputs, axis=-1, keepdims=True)
    center = inputs - middle
    spread = jnp.mean(center * center, axis=-1, keepdims=True)
    scaled = lax.rsqrt(spread + NORM_EPS)
    unit_rows = center * scaled
    return (unit_rows * gain_row + shift_row, unit_rows, scaled)


def norm_back(grad_in, unit_rows, scaled, gain_row):
    gain_grad = jnp.sum(grad_in * unit_rows, axis=(0, 1))
    shift_grad = jnp.sum(grad_in, axis=(0, 1))
    inner_grad = grad_in * gain_row
    centered = inner_grad - jnp.mean(inner_grad, axis=-1, keepdims=True)
    result = scaled * (
        centered - unit_rows * jnp.mean(inner_grad * unit_rows, axis=-1, keepdims=True)
    )
    return (result, gain_grad, shift_grad)


def gelu_both(inner_sum):
    normal_cdf = 0.5 * (1.0 + lax.erf(inner_sum * ROOT_HALF))
    density = jnp.exp(-0.5 * inner_sum * inner_sum) * DENSITY_SCALE
    return (inner_sum * normal_cdf, normal_cdf + inner_sum * density)


def split_tiles(key_rows, value_rows, key_valid):
    key_count = key_rows.shape[0]
    tile_width = 512
    tile_count = key_count // tile_width
    return (
        key_rows.reshape(tile_count, tile_width, H, HEAD),
        value_rows.reshape(tile_count, tile_width, H, HEAD),
        key_valid.reshape(tile_count, tile_width),
    )


def masked_scores(queries, key_tile, mask_tile):
    products = jnp.einsum("qhd,khd->hqk", queries, key_tile, preferred_element_type=jnp.float32)
    return jnp.where(mask_tile[None, None, :], products, NEG_FILL)


def attend_forward(queries, key_rows, value_rows, key_valid):
    key_tiles, value_tiles, mask_tiles = split_tiles(key_rows, value_rows, key_valid)
    row_span = queries.shape[0]

    def stats_step(running, portion):
        highest, summed = running
        key_tile, mask_tile = portion
        scores = masked_scores(queries, key_tile, mask_tile)
        new_peak = jnp.maximum(highest, jnp.max(scores, axis=-1))
        raised = jnp.where(mask_tile[None, None, :], jnp.exp(scores - new_peak[:, :, None]), 0.0)
        return ((new_peak, summed * jnp.exp(highest - new_peak) + jnp.sum(raised, axis=-1)), None)

    start_peak = jnp.full((H, row_span), NEG_FILL, jnp.float32)
    start_sum = jnp.zeros((H, row_span), jnp.float32)
    (highest, summed), _ = lax.scan(stats_step, (start_peak, start_sum), (key_tiles, mask_tiles))
    logsum = highest + jnp.log(summed)

    def value_step(running, portion):
        key_tile, value_tile, mask_tile = portion
        scores = masked_scores(queries, key_tile, mask_tile)
        prob_low = jnp.where(
            mask_tile[None, None, :], jnp.exp(scores - logsum[:, :, None]), 0.0
        ).astype(jnp.bfloat16)
        return (
            running
            + jnp.einsum("hqk,khd->qhd", prob_low, value_tile, preferred_element_type=jnp.float32),
            None,
        )

    attended, _ = lax.scan(
        value_step,
        jnp.zeros((row_span, H, HEAD), jnp.float32),
        (key_tiles, value_tiles, mask_tiles),
    )
    return (attended, logsum)


def attend_backward(
    queries, key_rows, value_rows, key_valid, logsum, delta_rows, grad_heads, with_keys
):
    key_tiles, value_tiles, mask_tiles = split_tiles(key_rows, value_rows, key_valid)

    def back_step(running, portion):
        key_tile, value_tile, mask_tile = portion
        scores = masked_scores(queries, key_tile, mask_tile)
        prob_rows = jnp.where(mask_tile[None, None, :], jnp.exp(scores - logsum[:, :, None]), 0.0)
        prob_grad = jnp.einsum(
            "qhd,khd->hqk", grad_heads, value_tile, preferred_element_type=jnp.float32
        )
        score_low = (prob_rows * (prob_grad - delta_rows[:, :, None])).astype(jnp.bfloat16)
        running = running + jnp.einsum(
            "hqk,khd->qhd", score_low, key_tile, preferred_element_type=jnp.float32
        )
        value_part = jnp.einsum(
            "hqk,qhd->khd",
            prob_rows.astype(jnp.bfloat16),
            grad_heads,
            preferred_element_type=jnp.float32,
        )
        key_part = jnp.einsum(
            "hqk,qhd->khd", score_low, queries, preferred_element_type=jnp.float32
        )
        return (running, (key_part, value_part))

    start_grad = jnp.zeros(queries.shape, jnp.float32)
    query_grad, pieces = lax.scan(back_step, start_grad, (key_tiles, value_tiles, mask_tiles))
    key_count = key_rows.shape[0]
    return (
        query_grad,
        pieces[0].reshape(key_count, H * HEAD),
        pieces[1].reshape(key_count, H * HEAD),
    )


def body(
    tokens,
    doc_lengths,
    group_deal,
    qkv_weight,
    out_weight,
    up_weight,
    up_bias,
    down_weight,
    proj_weight,
    vectors,
    cotangent,
):
    gathered = (
        lax.all_gather(qkv_weight, "wa", axis=0, tiled=True),
        lax.all_gather(out_weight, "wa", axis=0, tiled=True),
        lax.all_gather(up_weight, "wa", axis=0, tiled=True),
        lax.all_gather(up_bias, "wa", axis=0, tiled=True),
        lax.all_gather(down_weight, "wa", axis=0, tiled=True),
        lax.all_gather(proj_weight, "wa", axis=0, tiled=True),
        lax.all_gather(vectors, "wa", axis=1, tiled=True),
    )
    qkv_full, out_full, up_full, bias_full, down_full, proj_full, vector_full = gathered
    seq_count, group_rows, model_width = tokens.shape
    ctx_count = lax.axis_size("ctx")
    seq_start = lax.axis_index("wa") * seq_count
    my_lengths = lax.dynamic_slice_in_dim(doc_lengths, seq_start, seq_count, 0)
    my_deal = lax.dynamic_slice_in_dim(group_deal, seq_start, seq_count, 0)
    offsets = jnp.tile(jnp.arange(group_rows, dtype=jnp.int32), ctx_count)
    positions = jnp.repeat(my_deal, group_rows, axis=1) * group_rows + offsets[None, :]
    key_valid = positions < my_lengths[:, None]
    query_valid = lax.dynamic_slice_in_dim(
        key_valid, lax.axis_index("ctx") * group_rows, group_rows, 1
    )
    row_mask = query_valid.astype(jnp.float32)[:, :, None]
    query_scale = HEAD ** (-0.5)
    mixed_rows = jnp.einsum("scd,de->sce", tokens, qkv_full, preferred_element_type=jnp.float32)
    queries = ((mixed_rows[:, :, :model_width] + vector_full[0]) * query_scale).astype(jnp.bfloat16)
    key_rows = mixed_rows[:, :, model_width : 2 * model_width].astype(jnp.bfloat16)
    value_rows = (mixed_rows[:, :, 2 * model_width :] + vector_full[1]).astype(jnp.bfloat16)
    all_keys, all_values = (
        lax.all_gather(key_rows, "ctx", axis=1, tiled=True),
        lax.all_gather(value_rows, "ctx", axis=1, tiled=True),
    )
    query_heads = queries.reshape(seq_count, group_rows, H, HEAD)
    attended, logsum = jax.vmap(attend_forward)(query_heads, all_keys, all_values, key_valid)
    attended_low = attended.reshape(seq_count, group_rows, model_width).astype(jnp.bfloat16)
    first_sum = tokens.astype(jnp.float32) + (
        jnp.einsum("scd,de->sce", attended_low, out_full, preferred_element_type=jnp.float32)
        + vector_full[2]
    )
    normed, unit_one, scale_one = norm_rows(first_sum, vector_full[3], vector_full[4])
    normed_low = normed.astype(jnp.bfloat16)
    inner_sum = (
        jnp.einsum("scd,df->scf", normed_low, up_full, preferred_element_type=jnp.float32)
        + bias_full
    )
    active, gelu_slope = gelu_both(inner_sum)
    active_low = active.astype(jnp.bfloat16)
    second_sum = normed + (
        jnp.einsum("scf,fd->scd", active_low, down_full, preferred_element_type=jnp.float32)
        + vector_full[5]
    )
    final_sum, unit_two, scale_two = norm_rows(second_sum, vector_full[6], vector_full[7])
    final_low = final_sum.astype(jnp.bfloat16)
    project = jnp.einsum("scd,de->sce", final_low, proj_full, preferred_element_type=jnp.float32)
    inverse = lax.rsqrt(jnp.sum(project * project, axis=-1, keepdims=True) + NORM_EPS)
    direction = project * inverse
    embeddings = (direction * row_mask).astype(jnp.bfloat16)
    upstream = cotangent.astype(jnp.float32) * row_mask
    project_grad = (
        inverse * (upstream - direction * jnp.sum(upstream * direction, axis=-1, keepdims=True))
    ).astype(jnp.bfloat16)
    proj_grad = jnp.einsum(
        "scd,sce->de", final_low, project_grad, preferred_element_type=jnp.float32
    )
    final_grad = jnp.einsum(
        "sce,de->scd", project_grad, proj_full, preferred_element_type=jnp.float32
    )
    second_grad, gain_two, shift_two = norm_back(final_grad, unit_two, scale_two, vector_full[6])
    down_low = second_grad.astype(jnp.bfloat16)
    down_grad = jnp.einsum("scf,scd->fd", active_low, down_low, preferred_element_type=jnp.float32)
    inner_grad = (
        jnp.einsum("scd,fd->scf", down_low, down_full, preferred_element_type=jnp.float32)
        * gelu_slope
    )
    bias_grad = jnp.sum(inner_grad, axis=(0, 1))
    inner_low = inner_grad.astype(jnp.bfloat16)
    up_grad = jnp.einsum("scd,scf->df", normed_low, inner_low, preferred_element_type=jnp.float32)
    normed_grad = second_grad + jnp.einsum(
        "scf,df->scd", inner_low, up_full, preferred_element_type=jnp.float32
    )
    first_grad, gain_one, shift_one = norm_back(normed_grad, unit_one, scale_one, vector_full[3])
    first_low = first_grad.astype(jnp.bfloat16)
    out_grad = jnp.einsum(
        "scd,sce->de", attended_low, first_low, preferred_element_type=jnp.float32
    )
    attended_grad = jnp.einsum(
        "sce,de->scd", first_low, out_full, preferred_element_type=jnp.float32
    ).astype(jnp.bfloat16)
    grad_heads = attended_grad.reshape(seq_count, group_rows, H, HEAD)
    delta_rows = jnp.sum(grad_heads.astype(jnp.float32) * attended, axis=-1)
    delta_heads = jnp.swapaxes(delta_rows, 1, 2)
    query_grad, key_terms, value_terms = jax.vmap(partial(attend_backward, with_keys=True))(
        query_heads, all_keys, all_values, key_valid, logsum, delta_heads, grad_heads
    )
    key_grad, value_grad = (
        lax.psum_scatter(
            key_terms.astype(jnp.bfloat16), "ctx", scatter_dimension=1, tiled=True
        ).astype(jnp.float32),
        lax.psum_scatter(
            value_terms.astype(jnp.bfloat16), "ctx", scatter_dimension=1, tiled=True
        ).astype(jnp.float32),
    )
    query_part = (
        query_grad.reshape(seq_count, group_rows, model_width).astype(jnp.bfloat16) * query_scale
    )
    value_part = value_grad.astype(jnp.bfloat16)
    mixed_grad = jnp.concatenate([query_part, key_grad.astype(jnp.bfloat16), value_part], axis=-1)
    qkv_grad = jnp.einsum("scd,sce->de", tokens, mixed_grad, preferred_element_type=jnp.float32)
    tokens_grad = first_grad + jnp.einsum(
        "sce,de->scd", mixed_grad, qkv_full, preferred_element_type=jnp.float32
    )
    vectors_grad = jnp.stack(
        [
            jnp.sum(query_part.astype(jnp.float32), axis=(0, 1)),
            jnp.sum(value_part.astype(jnp.float32), axis=(0, 1)),
            jnp.sum(first_grad, axis=(0, 1)),
            gain_one,
            shift_one,
            jnp.sum(second_grad, axis=(0, 1)),
            gain_two,
            shift_two,
        ],
        axis=0,
    )
    owned = (
        lax.psum_scatter(
            qkv_grad.astype(jnp.bfloat16), "wa", scatter_dimension=0, tiled=True
        ).astype(jnp.float32),
        lax.psum_scatter(
            out_grad.astype(jnp.bfloat16), "wa", scatter_dimension=0, tiled=True
        ).astype(jnp.float32),
        lax.psum_scatter(
            up_grad.astype(jnp.bfloat16), "wa", scatter_dimension=0, tiled=True
        ).astype(jnp.float32),
        lax.psum_scatter(
            bias_grad.astype(jnp.bfloat16), "wa", scatter_dimension=0, tiled=True
        ).astype(jnp.float32),
        lax.psum_scatter(
            down_grad.astype(jnp.bfloat16), "wa", scatter_dimension=0, tiled=True
        ).astype(jnp.float32),
        lax.psum_scatter(
            proj_grad.astype(jnp.bfloat16), "wa", scatter_dimension=0, tiled=True
        ).astype(jnp.float32),
        lax.psum_scatter(
            vectors_grad.astype(jnp.bfloat16), "wa", scatter_dimension=1, tiled=True
        ).astype(jnp.float32),
    )
    summed = (
        lax.psum(owned[0].astype(jnp.bfloat16), "ctx").astype(jnp.float32),
        lax.psum(owned[1].astype(jnp.bfloat16), "ctx").astype(jnp.float32),
        lax.psum(owned[2].astype(jnp.bfloat16), "ctx").astype(jnp.float32),
        lax.psum(owned[3].astype(jnp.bfloat16), "ctx").astype(jnp.float32),
        lax.psum(owned[4].astype(jnp.bfloat16), "ctx").astype(jnp.float32),
        lax.psum(owned[5].astype(jnp.bfloat16), "ctx").astype(jnp.float32),
        lax.psum(owned[6].astype(jnp.bfloat16), "ctx").astype(jnp.float32),
    )
    return (
        embeddings,
        tokens_grad,
        summed[0],
        summed[1],
        summed[2],
        summed[3],
        summed[4],
        summed[5],
        summed[6],
    )


def solution(mesh):
    in_specs = (
        P("wa", "ctx", None),
        P(),
        P(),
        P("wa", None),
        P("wa", None),
        P("wa", None),
        P("wa"),
        P("wa", None),
        P("wa", None),
        P(None, "wa"),
        P("wa", "ctx", None),
    )
    out_specs = (
        P("wa", "ctx", None),
        P("wa", "ctx", None),
        P("wa", None),
        P("wa", None),
        P("wa", None),
        P("wa"),
        P("wa", None),
        P("wa", None),
        P(None, "wa"),
    )
    return jax.shard_map(body, mesh=mesh, in_specs=in_specs, out_specs=out_specs, check_vma=False)
```

profile of v0, /device:TPU:0, one launch (start us, length us, event | category | flops | bytes accessed | tf_op | source)
XLA Modules:
  0.0 944.5 jit_solution(11446303625677070540)
XLA Ops:
  8.0 15.1 %all-gather = bf16[4,192,8]{1,2,0:T(8,128)(2,1)S(1)} all-gather(bf16[1,192,8]{1,2,0:T(8,128)(2,1)} %bitcast.249), channel_id=1, replica_groups=mesh['ctx'=8,'wa'=4] {'wa'}, dimensions={0}, use_global_device_ids=true | all-gather | bytes 15360 | tf_op jit(solution)/shard_map/all_gather | solution.py:151
  23.8 58.5 %all-gather.9.cloned.1.call-done = bf16[768,2304]{1,0:T(8,128)(2,1)} async-done(((bf16[192,2304]{1,0:T(8,128)(2,1)}), bf16[768,2304]{1,0:T(8,128)(2,1)}) %all-gather.9.cloned.1.call-update) | async-done | bytes 3538960 | tf_op jit(solution)/shard_map/all_gather | solution.py:145
  82.3 3.2 fusion.81
  90.8 13.1 %all-gather.1 = bf16[4,1,768]{2,1,0:T(2,128)(2,1)S(1)} all-gather(bf16[1,1,768]{2,1,0:T(2,128)(2,1)S(1)} %reshape.193), channel_id=1, replica_groups=mesh['ctx'=8,'wa'=4] {'wa'}, dimensions={0}, use_global_device_ids=true | all-gather | bytes 7680 | tf_op jit(solution)/shard_map/all_gather | solution.py:148
  105.4 14.3 %all_gather.35 = bf16[768,128]{1,0:T(8,128)(2,1)} all-gather(bf16[192,128]{1,0:T(8,128)(2,1)S(1)} %copy-done.36), channel_id=1, replica_groups=mesh['ctx'=8,'wa'=4] {'wa'}, dimensions={0}, use_global_device_ids=true | all-gather | bytes 245760 | tf_op jit(solution)/shard_map/all_gather | solution.py:150
  120.6 3.2 copy.70
  123.8 4.0 reshape.179
  127.8 4.3 copy.75
  132.1 19.9 %all-gather.13.cloned.1.call-done = bf16[2,1024,768]{2,1,0:T(8,128)(2,1)} async-done(((bf16[2,128,768]{2,1,0:T(8,128)(2,1)}), bf16[2,1024,768]{2,1,0:T(8,128)(2,1)}) %all-gather.13.cloned.1.call-update) | async-done | bytes 3145744 | tf_op jit(solution)/shard_map/all_gather | solution.py:172
  152.0 3.2 copy.71
  155.2 4.0 reshape.180
  159.2 2.7 copy.77
  162.0 8.7 while.39
  172.0 11.2 %while.40 = (s32[]{:T(128)}, f32[2,128,12,64]{1,3,2,0:T(8,128)}, bf16[2,2,512,12,64]{2,4,3,1,0:T(8,128)(2,1)}, pred[2,2,512]{2,1,0:T(4,128)(4,1)}, bf16[2,2,512,...) while((s32[]{:T(128)}, f32[2,128,12,64]{1,3,2,0:T(8,128)}, ...), condition=%wide.region_5.6_spmd.clone, body=%wide.region_4.5_spmd.clone.sunk | while | flops 409337856 | bytes 5133938 | solution.py:86
  172.6 4.6 fusion.200
  177.9 4.8 fusion.200
  188.4 85.4 %all-gather.17.cloned.1.call-done = bf16[768,3072]{1,0:T(8,128)(2,1)} async-done(((bf16[192,3072]{1,0:T(8,128)(2,1)}), bf16[768,3072]{1,0:T(8,128)(2,1)}) %all-gather.17.cloned.1.call-update) | async-done | bytes 4718608 | tf_op jit(solution)/shard_map/all_gather | solution.py:147
  273.8 6.5 multiply_convert_fusion.1
  280.4 82.7 %all-gather.19.cloned.1.call-done = bf16[3072,768]{1,0:T(8,128)(2,1)} async-done(((bf16[768,768]{1,0:T(8,128)(2,1)}), bf16[3072,768]{1,0:T(8,128)(2,1)}) %all-gather.19.cloned.1.call-update) | async-done | bytes 4718608 | tf_op jit(solution)/shard_map/all_gather | solution.py:149
  363.1 4.5 fusion.155
  370.2 3.2 multiply_reduce_fusion
  376.6 7.2 fusion.158
  393.8 25.8 %while.41 = (s32[]{:T(128)}, f32[2,128,12,64]{1,3,2,0:T(8,128)}, bf16[2,2,512,12,64]{2,4,3,1,0:T(8,128)(2,1)}, bf16[2,2,512,12,64]{2,4,3,1,0:T(8,128)(2,1)}, bf1...) while((s32[]{:T(128)}, f32[2,128,12,64]{1,3,2,0:T(8,128)}, ...), condition=%wide.region_18.19_spmd.clone, body=%wide.region_17.18_spmd.clone.sunk | while | flops 1022754816 | bytes 113400248 | solution.py:122
  395.9 2.7 multiply_convert_fusion.4
  408.7 2.7 multiply_convert_fusion.4
  419.6 5.1 copy.87
  424.7 3.9 convert_element_type.275
  428.6 4.7 copy.88
  433.6 5.1 copy.85
  438.7 3.9 convert_element_type.272
  442.6 4.7 copy.86
  450.2 27.7 %reduce-scatter.15.cloned.1.call-done = bf16[2,128,768]{2,1,0:T(8,128)(2,1)} async-done(((bf16[2,1024,768]{2,1,0:T(8,128)(2,1)}), bf16[2,128,768]{2,1,0:T(8,128)(2,1)}) %reduce-scatter.15.cloned.1.call-update) | async-done | bytes 393232 | tf_op jit(solution)/shard_map/reduce_scatter | solution.py:241
  477.9 49.4 %reduce-scatter.13.cloned.1.call-done = bf16[2,128,768]{2,1,0:T(8,128)(2,1)} async-done(((bf16[2,1024,768]{2,1,0:T(8,128)(2,1)}), bf16[2,128,768]{2,1,0:T(8,128)(2,1)}) %reduce-scatter.13.cloned.1.call-update) | async-done | bytes 393232 | tf_op jit(solution)/shard_map/reduce_scatter | solution.py:238
  527.3 2.5 fusion.72
  529.8 4.0 copy.104
  536.7 4.5 bitcast_convert_fusion.1
  542.8 3.6 bitcast_convert_fusion
  550.7 49.9 %reduce-scatter.25.cloned.1.call-done = bf16[192,2304]{1,0:T(8,128)(2,1)} async-done(((bf16[768,2304]{1,0:T(8,128)(2,1)}), bf16[192,2304]{1,0:T(8,128)(2,1)}) %reduce-scatter.25.cloned.1.call-update) | async-done | bytes 884752
  602.9 29.9 %reduce-scatter.17.cloned.1.call-done = bf16[192,768]{1,0:T(8,128)(2,1)} async-done(((bf16[768,768]{1,0:T(8,128)(2,1)}), bf16[192,768]{1,0:T(8,128)(2,1)}) %reduce-scatter.17.cloned.1.call-update) | async-done | bytes 294928 | tf_op jit(solution)/shard_map/reduce_scatter | solution.py:271
  632.8 86.2 %reduce-scatter.19.cloned.1.call-done = bf16[192,3072]{1,0:T(8,128)(2,1)} async-done(((bf16[768,3072]{1,0:T(8,128)(2,1)}), bf16[192,3072]{1,0:T(8,128)(2,1)}) %reduce-scatter.19.cloned.1.call-update) | async-done | bytes 1179664 | tf_op jit(solution)/shard_map/reduce_scatter | solution.py:274
  719.0 88.0 %reduce-scatter.21.cloned.1.call-done = bf16[768,768]{1,0:T(8,128)(2,1)} async-done(((bf16[3072,768]{1,0:T(8,128)(2,1)}), bf16[768,768]{1,0:T(8,128)(2,1)}) %reduce-scatter.21.cloned.1.call-update) | async-done | bytes 1179664 | tf_op jit(solution)/shard_map/reduce_scatter | solution.py:280
  809.1 11.1 %all-reduce = bf16[3072]{0:T(1024)(128)(2,1)S(1)} all-reduce(bf16[3072]{0:T(1024)(128)(2,1)S(1)} %copy-done.54), channel_id=7, replica_groups=mesh['ctx'=8,'wa'=4] {'wa'}, use_global_device_ids=true, to_apply=%region_28.29.clone | all-reduce | flops 3072 | bytes 12288
  820.3 4.0 fusion.88
  824.3 5.8 reduce-scatter.27.cloned.1.call-done
  830.9 19.6 %reduce-scatter.23.cloned.1.call-done = bf16[192,128]{1,0:T(8,128)(2,1)} async-done(((bf16[768,128]{1,0:T(8,128)(2,1)}), bf16[192,128]{1,0:T(8,128)(2,1)}) %reduce-scatter.23.cloned.1.call-update) | async-done | bytes 49168 | tf_op jit(solution)/shard_map/reduce_scatter | solution.py:283
  850.5 24.6 %all-reduce.1 = (bf16[768]{0:T(1024)(128)(2,1)S(1)}, bf16[192,128]{1,0:T(8,128)(2,1)S(1)}, bf16[8,192]{1,0:T(8,128)(2,1)S(1)}) all-reduce(bf16[768]{0:T(1024)(128)(2,1)S(1)} %dynamic-slice.1, bf16[192,128]{1,0:T(8,128)(2,1)} %reduce-scatter.23.cloned.1.call-done, bf16[8,192]{1,0:T(8,128)(2,1)S(1)} %copy.107), channel_id=1, replica_groups=mesh['ctx'=8,'wa'=4] {'ctx'}, use_global_device_ids=true, to_apply=%region_29.30 | all-reduce | flops 26880 | bytes 107520 | tf_op jit(solution)/shard_map/psum | solution.py:294
  877.0 54.0 %all-reduce.5.cloned.1.call-done = (bf16[192,2304]{0,1:T(8,128)(2,1)}, bf16[192,768]{1,0:T(8,128)(2,1)}, bf16[192,3072]{1,0:T(8,128)(2,1)}, bf16[768,768]{1,0:T(8,128)(2,1)}) async-done(((bf16[192,2304]{0,1:T(8,128)(2,1)}, bf16[192,768]{1,0:T(8,128)(2,1)}, bf16[192,3072]{1,0:T(8,128)(2,1)}, bf16[768,768]{1,0:T(8,128)(2,1)}), (bf16[192,2304]{0,1:T(8,128)(2,1)}, bf16[192,768]{1,0:T(8,128)(2,1)}, ...) | async-done | bytes 3538960 | tf_op jit(solution)/shard_map/psum | solution.py:291
  931.0 2.6 copy.96
  (290 shorter events, 82.9 us)
Async XLA Ops:
  7.2 75.1 %all-gather.9.cloned.1.call-start = ((), (), s32[]{:S(2)}) async-start(), calls=%async_computation.8 | async-start | bytes 4423680 | tf_op jit(solution)/shard_map/all_gather | solution.py:145
  7.9 112.7 %all-gather.11.cloned.1.call-start = ((), (), s32[]{:S(2)}) async-start(), calls=%async_computation.9 | async-start | bytes 3538944 | tf_op jit(solution)/shard_map/all_gather | solution.py:173
  85.5 3.7 copy-start.57
  85.5 3.7 copy-start.63
  85.5 19.0 %copy-start.35 = (bf16[2,128,128]{2,1,0:T(8,128)(2,1)S(1)}, bf16[2,128,128]{2,1,0:T(8,128)(2,1)}, u32[]{:S(2)}) copy-start(bf16[2,128,128]{2,1,0:T(8,128)(2,1)} %param.27) | copy-start | bytes 196612
  85.5 19.9 %copy-start.36 = (bf16[192,128]{1,0:T(8,128)(2,1)S(1)}, bf16[192,128]{1,0:T(8,128)(2,1)}, u32[]{:S(2)}) copy-start(bf16[192,128]{1,0:T(8,128)(2,1)} %param.25) | copy-start | bytes 147460
  86.4 65.6 %all-gather.13.cloned.1.call-start = ((), (), s32[]{:S(2)}) async-start(), calls=%async_computation.10 | async-start | bytes 3538944 | tf_op jit(solution)/shard_map/all_gather | solution.py:172
  87.3 97.9 %all-gather.15.cloned.1.call-start = ((), (), s32[]{:S(2)}) async-start(), calls=%async_computation.11 | async-start | bytes 1474560 | tf_op jit(solution)/shard_map/all_gather | solution.py:146
  87.9 185.9 %all-gather.17.cloned.1.call-start = ((), (), s32[]{:S(2)}) async-start(), calls=%async_computation.12 | async-start | bytes 5898240 | tf_op jit(solution)/shard_map/all_gather | solution.py:147
  88.4 274.6 %all-gather.19.cloned.1.call-start = ((), (), s32[]{:S(2)}) async-start(), calls=%async_computation.13 | async-start | bytes 5898240 | tf_op jit(solution)/shard_map/all_gather | solution.py:149
  89.0 388.9 %reduce-scatter.15.cloned.1.call-start = ((), (), s32[]{:S(2)}) async-start(), calls=%async_computation.15 | async-start | bytes 3538944 | tf_op jit(solution)/shard_map/reduce_scatter | solution.py:241
  172.0 13.2 %copy-start.45 = (f32[768]{0:T(1024)S(1)}, f32[768]{0:T(1024)}, u32[]{:S(2)}) copy-start(f32[768]{0:T(1024)} %get-tuple-element.337) | copy-start | bytes 9220
  183.2 90.6 %copy-start.33 = (f32[768]{0:T(1024)S(1)}, f32[768]{0:T(1024)}, u32[]{:S(2)}) copy-start(f32[768]{0:T(1024)} %get-tuple-element.336) | copy-start | bytes 9220
  183.2 90.6 %copy-start.34 = (f32[768]{0:T(1024)S(1)}, f32[768]{0:T(1024)}, u32[]{:S(2)}) copy-start(f32[768]{0:T(1024)} %get-tuple-element.335) | copy-start | bytes 9220
  187.3 196.5 %copy-start.38 = (f32[2,128]{1,0:T(2,128)}, f32[2,128]{1,0:T(2,128)S(1)}, u32[]{:S(2)}) copy-start(f32[2,128]{1,0:T(2,128)S(1)} %broadcast_multiply_fusion.5) | copy-start | bytes 3076
  188.4 92.0 %copy-start.48 = (f32[2,128]{1,0:T(2,128)}, f32[2,128]{1,0:T(2,128)S(1)}, u32[]{:S(2)}) copy-start(f32[2,128]{1,0:T(2,128)S(1)} %add_rsqrt_fusion.2) | copy-start | bytes 3076
  363.1 5.5 copy-start.25
  363.1 5.5 copy-start.37
  363.1 5.5 copy-start.43
  374.2 9.6 %slice-start = ((s8[4718592]{0:T(1024)(128)(4,1)}), s8[4194304]{0:T(1024)(128)(4,1)S(1)}, s32[]{:S(2)}) async-start(s8[4718592]{0:T(1024)(128)(4,1)} %bitcast.250), calls=%async_computation.23 | async-start | bytes 8388608
  376.6 7.2 copy-start.18
  376.6 7.2 copy-start.4
  376.6 7.3 copy-start.49
  376.6 7.3 slice-start.1
  383.8 4.8 copy-start.10
  386.2 7.6 copy-start.31
  395.9 2.8 copy-start.13
  400.8 3.0 copy-start.15
  408.7 2.8 copy-start.13
  413.6 3.0 copy-start.15
  433.3 94.0 %reduce-scatter.13.cloned.1.call-start = ((), (), s32[]{:S(2)}) async-start(), calls=%async_computation.14 | async-start | bytes 3538944 | tf_op jit(solution)/shard_map/reduce_scatter | solution.py:238
  447.3 153.2 %reduce-scatter.25.cloned.1.call-start = ((), (), s32[]{:S(2)}) async-start(), calls=%async_computation.20 | async-start | bytes 4423680
  533.8 2.8 copy-start.5
  533.9 2.8 copy-start.22
  533.9 2.8 copy-start.39
  533.9 98.9 %reduce-scatter.17.cloned.1.call-start = ((), (), s32[]{:S(2)}) async-start(), calls=%async_computation.16 | async-start | bytes 1474560 | tf_op jit(solution)/shard_map/reduce_scatter | solution.py:271
  536.6 182.4 %reduce-scatter.19.cloned.1.call-start = ((), (), s32[]{:S(2)}) async-start(), calls=%async_computation.17 | async-start | bytes 5898240 | tf_op jit(solution)/shard_map/reduce_scatter | solution.py:274
  541.2 265.9 %reduce-scatter.21.cloned.1.call-start = ((), (), s32[]{:S(2)}) async-start(), calls=%async_computation.18 | async-start | bytes 5898240 | tf_op jit(solution)/shard_map/reduce_scatter | solution.py:280
  546.5 283.5 %reduce-scatter.27.cloned.1.call-start = ((), (), s32[]{:S(2)}) async-start(), calls=%async_computation.21 | async-start | bytes 245760
  548.4 302.1 %reduce-scatter.23.cloned.1.call-start = ((), (), s32[]{:S(2)}) async-start(), calls=%async_computation.19 | async-start | bytes 245760 | tf_op jit(solution)/shard_map/reduce_scatter | solution.py:283
  550.6 256.5 %copy-start.64 = (u32[32]{0:T(128)S(1)}, u32[32]{0:T(128)}, u32[]{:S(2)}) copy-start(u32[32]{0:T(128)} %constant.101) | copy-start | bytes 388
  550.6 258.5 %copy-start.54 = (bf16[3072]{0:T(1024)(128)(2,1)S(1)}, bf16[3072]{0:T(1024)(128)(2,1)}, u32[]{:S(2)}) copy-start(bf16[3072]{0:T(1024)(128)(2,1)} %get-tuple-element.415) | copy-start | bytes 18436
  550.6 269.7 %copy-start.30 = (bf16[2,128,768]{2,1,0:T(8,128)(2,1)S(1)}, bf16[2,128,768]{2,1,0:T(8,128)(2,1)}, u32[]{:S(2)}) copy-start(bf16[2,128,768]{2,1,0:T(8,128)(2,1)} %copy.89) | copy-start | bytes 1179652
  550.6 269.6 %copy-start.62 = (bf16[2,128,768]{2,1,0:T(8,128)(2,1)S(1)}, bf16[2,128,768]{2,1,0:T(8,128)(2,1)}, u32[]{:S(2)}) copy-start(bf16[2,128,768]{2,1,0:T(8,128)(2,1)} %reduce-scatter.13.cloned.1.call-done) | copy-start | bytes 1179652
  550.6 380.4 %all-reduce.5.cloned.1.call-start = ((), (), s32[]{:S(2)}) async-start(), calls=%async_computation.22 | async-start | bytes 7667712 | tf_op jit(solution)/shard_map/psum | solution.py:291
  931.0 2.6 copy-start.32
  931.0 3.5 copy-start.24
  931.0 5.2 copy-start.23
  (46 other events, 69.0 us)
Sparse Core Ops, SparseCore 0:
  9.6 72.6 all-gather.8
  86.5 30.7 all-gather.10
  119.8 32.1 all-gather.12
  153.4 30.2 all-gather.14
  185.2 88.6 all-gather.16
  275.2 87.7 all-gather.18
  433.4 44.4 reduce-scatter.14
  481.3 46.0 reduce-scatter.12
  534.0 66.4 reduce-scatter.24
  603.3 29.4 reduce-scatter.16
  635.1 83.8 reduce-scatter.18
  721.2 85.7 reduce-scatter.20
  809.9 20.1 reduce-scatter.26
  832.7 17.7 reduce-scatter.22
  854.7 76.2 all-reduce.4
where the time goes:
time: 953 us; the launch traced here: 945 us
  waiting for transfers between devices  660 us (69%)
  local copies, waits for them, and re-layouts  86.5 us (9%)
  matrix products  78.4 us (8%)
  blocking collectives  78.2 us (8%)
  other arithmetic  24.5 us (3%)
  between operations  15.5 us (2%)
    reduce_scatter x1, waiting for transfers between devices, body(): lax.psum_scatter(down_grad.astype(jnp.bfloat16), 'wa', scatter_dimension=...  88 us
    reduce_scatter x1, waiting for transfers between devices, body(): lax.psum_scatter(up_grad.astype(jnp.bfloat16), 'wa', scatter_dimension=0,...  86.2 us
    all_gather x1, waiting for transfers between devices, body(): lax.all_gather(up_weight, 'wa', axis=0, tiled=True)  85.4 us
    all_gather x1, waiting for transfers between devices, body(): lax.all_gather(down_weight, 'wa', axis=0, tiled=True)  82.7 us
    all_gather x1, waiting for transfers between devices, body(): lax.all_gather(qkv_weight, 'wa', axis=0, tiled=True)  58.5 us
    unnamed x17, waiting for transfers between devices  58.1 us
    psum x1, waiting for transfers between devices, body(): lax.psum(owned[0].astype(jnp.bfloat16), 'ctx').astype(jnp.float32)  54 us
    reduce_scatter x1, waiting for transfers between devices, body(): lax.psum_scatter(key_terms.astype(jnp.bfloat16), 'ctx', scatter_dimension...  49.4 us
  transfers between devices with their start and end apart: 15, of which 13 were waited for; matrix products, arithmetic and copies ran while one was open for 10% of the time, Pallas kernels for 0%

commit v1 on v0

--- a/solution.py
+++ b/solution.py
@@ -10,6 +10,19 @@
 NORM_EPS = 1e-06
 ROOT_HALF = 0.7071067811865476
 DENSITY_SCALE = 0.3989422804014327
+
+
+def ring_gather(shard, axis, dim):
+    ways = lax.axis_size(axis)
+    up = [(d, (d + 1) % ways) for d in range(ways)]
+    down = [(d, (d - 1) % ways) for d in range(ways)]
+    earlier, later = ([shard], [shard])
+    for _ in range(ways // 2):
+        earlier.append(lax.ppermute(earlier[-1], axis, up))
+    for _ in range((ways - 1) // 2):
+        later.append(lax.ppermute(later[-1], axis, down))
+    line = jnp.concatenate([*earlier[::-1], *later[1:]], axis=dim)
+    return jnp.roll(line, (lax.axis_index(axis) - ways // 2) * shard.shape[dim], axis=dim)
 
 
 def norm_rows(inputs, gain_row, shift_row):
@@ -146,7 +159,7 @@
         lax.all_gather(out_weight, "wa", axis=0, tiled=True),
         lax.all_gather(up_weight, "wa", axis=0, tiled=True),
         lax.all_gather(up_bias, "wa", axis=0, tiled=True),
-        lax.all_gather(down_weight, "wa", axis=0, tiled=True),
+        ring_gather(down_weight, "wa", 0),
         lax.all_gather(proj_weight, "wa", axis=0, tiled=True),
         lax.all_gather(vectors, "wa", axis=1, tiled=True),
     )

time: 953 us -> 909 us (0.954)
  waiting for transfers between devices: 660 us -> 516 us
  blocking collectives: 78.2 us -> 132 us
  matrix products: 78.4 us -> 95.8 us
  local copies, waits for them, and re-layouts: 86.5 us -> 103 us
    all_gather x1, waiting for transfers between devices: 85.4 us -> 0.02 us  [body(): lax.all_gather(up_weight, 'wa', axis=0, tiled=True)]
    all_gather x1 -> x0, waiting for transfers between devices: 82.7 us -> none  [body(): lax.all_gather(down_weight, 'wa', axis=0, tiled=True)]
    all_gather x1, blocking collectives: 13.1 us -> 64.3 us  [body(): lax.all_gather(up_bias, 'wa', axis=0, tiled=True)]
    ppermute x0 -> x3, waiting for transfers between devices: none -> 26.7 us  [the longest x2 26.7 us: ring_gather(): earlier.append(lax.ppermute(earlier[-1], axis, up))]
    all_gather x1, waiting for transfers between devices: 19.9 us -> 0.02 us  [body(): lax.all_gather(key_rows, 'ctx', axis=1, tiled=True)]
    all_gather x1, waiting for transfers between devices: 58.5 us -> 74.3 us  [body(): lax.all_gather(qkv_weight, 'wa', axis=0, tiled=True)]
    unnamed x126 -> x141, local copies, waits for them, and re-layouts: 27.6 us -> 37.2 us
    unnamed x17 -> x16, waiting for transfers between devices: 58.1 us -> 56.7 us
  transfers between devices with their start and end apart: 15 -> 17, of which waited for: 13 -> 11; matrix products, arithmetic and copies ran while one was open for 10% -> 13% of each run, Pallas kernels for 0% -> 0%
where the time goes in v1:
time: 909 us; the launch traced here: 900 us
  waiting for transfers between devices  516 us (57%)
  blocking collectives  132 us (15%)
  local copies, waits for them, and re-layouts  103 us (11%)
  matrix products  95.8 us (11%)
  other arithmetic  32.5 us (4%)
  between operations  15.7 us (2%)
    reduce_scatter x1, waiting for transfers between devices, body(): lax.psum_scatter(down_grad.astype(jnp.bfloat16), 'wa', scatter_dimension=...  88.2 us
    reduce_scatter x1, waiting for transfers between devices, body(): lax.psum_scatter(up_grad.astype(jnp.bfloat16), 'wa', scatter_dimension=0,...  86.1 us
    all_gather x1, waiting for transfers between devices, body(): lax.all_gather(qkv_weight, 'wa', axis=0, tiled=True)  74.3 us
    all_gather x1, blocking collectives, body(): lax.all_gather(up_bias, 'wa', axis=0, tiled=True)  64.3 us
    unnamed x16, waiting for transfers between devices  56.7 us
    psum x1, waiting for transfers between devices, body(): lax.psum(owned[0].astype(jnp.bfloat16), 'ctx').astype(jnp.float32)  54.1 us
    reduce_scatter x1, waiting for transfers between devices, body(): lax.psum_scatter(key_terms.astype(jnp.bfloat16), 'ctx', scatter_dimension...  49.5 us
    unnamed x141, local copies, waits for them, and re-layouts  37.2 us
  transfers between devices with their start and end apart: 17, of which 11 were waited for; matrix products, arithmetic and copies ran while one was open for 13% of the time, Pallas kernels for 0%

profile of v1, /device:TPU:0, one launch (start us, length us, event | category | flops | bytes accessed | tf_op | source)
XLA Modules:
  0.0 899.7 jit_solution(9968083897276049326)
XLA Ops:
  8.0 74.3 %all-gather.8.cloned.1.call-done = bf16[768,2304]{1,0:T(8,128)(2,1)} async-done(((bf16[192,2304]{1,0:T(8,128)(2,1)}), bf16[768,2304]{1,0:T(8,128)(2,1)}) %all-gather.8.cloned.1.call-update) | async-done | bytes 3538960 | tf_op jit(solution)/shard_map/all_gather | solution.py:158
  82.2 3.2 fusion.83
  86.3 13.2 %all-gather = bf16[4,192,8]{1,2,0:T(8,128)(2,1)S(1)} all-gather(bf16[1,192,8]{1,2,0:T(8,128)(2,1)S(1)} %bitcast.248), channel_id=1, replica_groups=mesh['ctx'=8,'wa'=4] {'wa'}, dimensions={0}, use_global_device_ids=true | all-gather | bytes 15360 | tf_op jit(solution)/shard_map/all_gather | solution.py:164
  103.4 26.6 %collective-permute-done = bf16[768,768]{1,0:T(8,128)(2,1)S(1)} collective-permute-done((bf16[768,768]{1,0:T(8,128)(2,1)S(1)}, bf16[768,768]{1,0:T(8,128)(2,1)S(1)}, u32[]{:S(2)}, u32[]{:S(2)}) %collective-permute-start) | collective-permute-done | bytes 1179680 | tf_op jit(solution)/shard_map/ppermute | solution.py:21
  130.0 3.8 collective-permute-start.2
  142.5 64.3 %all-gather.1 = bf16[4,1,768]{2,1,0:T(2,128)(2,1)S(1)} all-gather(bf16[1,1,768]{2,1,0:T(2,128)(2,1)S(1)} %reshape.193), channel_id=1, replica_groups=mesh['ctx'=8,'wa'=4] {'wa'}, dimensions={0}, use_global_device_ids=true | all-gather | bytes 7680 | tf_op jit(solution)/shard_map/all_gather | solution.py:161
  210.5 18.2 %all_gather.31 = bf16[768,128]{1,0:T(8,128)(2,1)} all-gather(bf16[192,128]{1,0:T(8,128)(2,1)} %param.25), channel_id=1, replica_groups=mesh['ctx'=8,'wa'=4] {'wa'}, dimensions={0}, use_global_device_ids=true | all-gather | bytes 245760 | tf_op jit(solution)/shard_map/all_gather | solution.py:163
  233.3 3.6 copy-done.37
  240.4 4.0 reshape.180
  247.0 4.7 copy.70
  251.7 6.2 reshape.179
  257.9 4.3 copy.75
  262.2 21.5 %while.39 = (s32[]{:T(128)}, f32[2,12,128]{2,1,0:T(8,128)S(1)}, f32[2,12,128]{2,1,0:T(8,128)}, pred[2,2,512]{2,1,0:T(4,128)(4,1)}, bf16[2,2,512,12,64]{2,4,3,1,0...) while((s32[]{:T(128)}, f32[2,12,128]{2,1,0:T(8,128)S(1)}, ...), condition=%wide.region_3.4_spmd.clone, body=%wide.region_0.3_spmd.clone.sunk | while | flops 210779136 | bytes 14816444 | solution.py:84
  262.8 4.7 bitcast_reduce_fusion.2
  268.2 4.0 fusion.199
  273.6 4.7 bitcast_reduce_fusion.2
  279.0 4.0 fusion.199
  285.0 11.2 %while.40 = (s32[]{:T(128)}, f32[2,128,12,64]{1,3,2,0:T(8,128)}, bf16[2,2,512,12,64]{2,4,3,1,0:T(8,128)(2,1)}, pred[2,2,512]{2,1,0:T(4,128)(4,1)}, bf16[2,2,512,...) while((s32[]{:T(128)}, f32[2,128,12,64]{1,3,2,0:T(8,128)}, ...), condition=%wide.region_5.6_spmd.clone, body=%wide.region_4.5_spmd.clone.sunk | while | flops 409337856 | bytes 5133419 | solution.py:99
  285.6 4.6 fusion.204
  290.9 4.8 fusion.204
  301.5 6.1 multiply_convert_fusion.1
  307.6 4.7 fusion.159
  321.2 8.2 fusion.162
  338.7 33.7 %while.41 = (s32[]{:T(128)}, f32[2,128,12,64]{1,3,2,0:T(8,128)}, bf16[2,2,512,12,64]{2,4,3,1,0:T(8,128)(2,1)}, bf16[2,2,512,12,64]{2,4,3,1,0:T(8,128)(2,1)}, bf1...) while((s32[]{:T(128)}, f32[2,128,12,64]{1,3,2,0:T(8,128)}, ...), condition=%wide.region_18.19_spmd.clone, body=%wide.region_17.18_spmd.clone.sunk | while | flops 1022754816 | bytes 132275064 | solution.py:135
  351.5 3.9 bitcast_dynamic-update-slice_fusion.5
  364.9 3.4 fusion.216
  368.4 4.0 bitcast_dynamic-update-slice_fusion.5
  372.4 5.1 copy.87
  377.5 3.9 convert_element_type.275
  381.4 4.6 copy.88
  386.1 5.1 copy.85
  391.3 4.1 convert_element_type.272
  395.4 4.8 copy.86
  402.4 30.1 %reduce-scatter.15.cloned.1.call-done = bf16[2,128,768]{2,1,0:T(8,128)(2,1)} async-done(((bf16[2,1024,768]{2,1,0:T(8,128)(2,1)}), bf16[2,128,768]{2,1,0:T(8,128)(2,1)}) %reduce-scatter.15.cloned.1.call-update) | async-done | bytes 393232 | tf_op jit(solution)/shard_map/reduce_scatter | solution.py:254
  432.5 49.5 %reduce-scatter.13.cloned.1.call-done = bf16[2,128,768]{2,1,0:T(8,128)(2,1)} async-done(((bf16[2,1024,768]{2,1,0:T(8,128)(2,1)}), bf16[2,128,768]{2,1,0:T(8,128)(2,1)}) %reduce-scatter.13.cloned.1.call-update) | async-done | bytes 393232 | tf_op jit(solution)/shard_map/reduce_scatter | solution.py:251
  484.5 4.0 copy.104
  491.3 4.5 bitcast_convert_fusion.1
  497.4 3.6 bitcast_convert_fusion
  505.4 49.8 %reduce-scatter.25.cloned.1.call-done = bf16[192,2304]{1,0:T(8,128)(2,1)} async-done(((bf16[768,2304]{1,0:T(8,128)(2,1)}), bf16[192,2304]{1,0:T(8,128)(2,1)}) %reduce-scatter.25.cloned.1.call-update) | async-done | bytes 884752
  557.5 30.1 %reduce-scatter.17.cloned.1.call-done = bf16[192,768]{1,0:T(8,128)(2,1)} async-done(((bf16[768,768]{1,0:T(8,128)(2,1)}), bf16[192,768]{1,0:T(8,128)(2,1)}) %reduce-scatter.17.cloned.1.call-update) | async-done | bytes 294928 | tf_op jit(solution)/shard_map/reduce_scatter | solution.py:284
  587.6 86.1 %reduce-scatter.19.cloned.1.call-done = bf16[192,3072]{1,0:T(8,128)(2,1)} async-done(((bf16[768,3072]{1,0:T(8,128)(2,1)}), bf16[192,3072]{1,0:T(8,128)(2,1)}) %reduce-scatter.19.cloned.1.call-update) | async-done | bytes 1179664 | tf_op jit(solution)/shard_map/reduce_scatter | solution.py:287
  673.7 88.2 %reduce-scatter.21.cloned.1.call-done = bf16[768,768]{1,0:T(8,128)(2,1)} async-done(((bf16[3072,768]{1,0:T(8,128)(2,1)}), bf16[768,768]{1,0:T(8,128)(2,1)}) %reduce-scatter.21.cloned.1.call-update) | async-done | bytes 1179664 | tf_op jit(solution)/shard_map/reduce_scatter | solution.py:293
  763.9 11.2 %all-reduce = bf16[3072]{0:T(1024)(128)(2,1)S(1)} all-reduce(bf16[3072]{0:T(1024)(128)(2,1)S(1)} %copy-done.57), channel_id=7, replica_groups=mesh['ctx'=8,'wa'=4] {'wa'}, use_global_device_ids=true, to_apply=%region_28.29.clone | all-reduce | flops 3072 | bytes 12288
  775.2 4.0 fusion.96
  779.2 5.5 reduce-scatter.27.cloned.1.call-done
  785.5 19.8 %reduce-scatter.23.cloned.1.call-done = bf16[192,128]{1,0:T(8,128)(2,1)} async-done(((bf16[768,128]{1,0:T(8,128)(2,1)}), bf16[192,128]{1,0:T(8,128)(2,1)}) %reduce-scatter.23.cloned.1.call-update) | async-done | bytes 49168 | tf_op jit(solution)/shard_map/reduce_scatter | solution.py:296
  805.4 24.6 %all-reduce.1 = (bf16[768]{0:T(1024)(128)(2,1)S(1)}, bf16[192,128]{1,0:T(8,128)(2,1)S(1)}, bf16[8,192]{1,0:T(8,128)(2,1)S(1)}) all-reduce(bf16[768]{0:T(1024)(128)(2,1)S(1)} %dynamic-slice.1, bf16[192,128]{1,0:T(8,128)(2,1)} %reduce-scatter.23.cloned.1.call-done, bf16[8,192]{1,0:T(8,128)(2,1)S(1)} %copy.107), channel_id=1, replica_groups=mesh['ctx'=8,'wa'=4] {'ctx'}, use_global_device_ids=true, to_apply=%region_29.30 | all-reduce | flops 26880 | bytes 107520 | tf_op jit(solution)/shard_map/psum | solution.py:307
  831.8 54.1 %all-reduce.5.cloned.1.call-done = (bf16[192,2304]{0,1:T(8,128)(2,1)}, bf16[192,768]{1,0:T(8,128)(2,1)}, bf16[192,3072]{1,0:T(8,128)(2,1)}, bf16[768,768]{1,0:T(8,128)(2,1)}) async-done(((bf16[192,2304]{0,1:T(8,128)(2,1)}, bf16[192,768]{1,0:T(8,128)(2,1)}, bf16[192,3072]{1,0:T(8,128)(2,1)}, bf16[768,768]{1,0:T(8,128)(2,1)}), (bf16[192,2304]{0,1:T(8,128)(2,1)}, bf16[192,768]{1,0:T(8,128)(2,1)}, ...) | async-done | bytes 3538960 | tf_op jit(solution)/shard_map/psum | solution.py:304
  (305 shorter events, 107.0 us)
Async XLA Ops:
  7.2 75.1 %all-gather.8.cloned.1.call-start = ((), (), s32[]{:S(2)}) async-start(), calls=%async_computation.8 | async-start | bytes 4423680 | tf_op jit(solution)/shard_map/all_gather | solution.py:158
  7.9 78.4 %copy-start.61 = (bf16[8,192]{1,0:T(8,128)(2,1)S(1)}, bf16[8,192]{1,0:T(8,128)(2,1)}, u32[]{:S(2)}) copy-start(bf16[8,192]{1,0:T(8,128)(2,1)} %param.26) | copy-start | bytes 9220
  7.9 229.3 %all-gather.12.cloned.1.call-start = ((), (), s32[]{:S(2)}) async-start(), calls=%async_computation.10 | async-start | bytes 3538944 | tf_op jit(solution)/shard_map/all_gather | solution.py:185
  85.5 17.8 %copy-start.13 = (bf16[768,768]{1,0:T(8,128)(2,1)S(1)}, bf16[768,768]{1,0:T(8,128)(2,1)}, u32[]{:S(2)}) copy-start(bf16[768,768]{1,0:T(8,128)(2,1)} %param.24) | copy-start | bytes 3538948
  86.3 160.7 %all-gather.10.cloned.1.call-start = ((), (), s32[]{:S(2)}) async-start(), calls=%async_computation.9 | async-start | bytes 3538944 | tf_op jit(solution)/shard_map/all_gather | solution.py:186
  102.6 195.5 %all-gather.14.cloned.1.call-start = ((), (), s32[]{:S(2)}) async-start(), calls=%async_computation.11 | async-start | bytes 1474560 | tf_op jit(solution)/shard_map/all_gather | solution.py:159
  103.2 198.2 %all-gather.16.cloned.1.call-start = ((), (), s32[]{:S(2)}) async-start(), calls=%async_computation.12 | async-start | bytes 5898240 | tf_op jit(solution)/shard_map/all_gather | solution.py:160
  103.3 26.7 %collective-permute-start = (bf16[768,768]{1,0:T(8,128)(2,1)S(1)}, bf16[768,768]{1,0:T(8,128)(2,1)S(1)}, u32[]{:S(2)}, u32[]{:S(2)}) collective-permute-start(bf16[768,768]{1,0:T(8,128)(2,1)S(1)} %copy-done.13), channel_id=1, source_target_pairs={{0,1},{1,2},{2,3},{3,0},{4,5},{5,6},{6,7},{7,4},{8,9},{9,10},{10,1... | collective-permute-start | bytes 3538952 | tf_op jit(solution)/shard_map/ppermute | solution.py:21
  130.0 100.1 %collective-permute-start.1 = (bf16[768,768]{1,0:T(8,128)(2,1)S(1)}, bf16[768,768]{1,0:T(8,128)(2,1)}, u32[]{:S(2)}, u32[]{:S(2)}) collective-permute-start(bf16[768,768]{1,0:T(8,128)(2,1)S(1)} %collective-permute-done), channel_id=1, source_target_pairs={{0,1},{1,2},{2,3},{3,0},{4,5},{5,6},{6,7},{7,4},{8,9},{9,10},{10,1... | collective-permute-start | bytes 3538952 | tf_op jit(solution)/shard_map/ppermute | solution.py:21
  130.0 101.6 %collective-permute-start.2 = (bf16[768,768]{1,0:T(8,128)(2,1)S(1)}, bf16[768,768]{1,0:T(8,128)(2,1)S(1)}, u32[]{:S(2)}, u32[]{:S(2)}) collective-permute-start(bf16[768,768]{1,0:T(8,128)(2,1)S(1)} %copy-done.13), channel_id=1, source_target_pairs={{0,3},{1,0},{2,1},{3,2},{4,7},{5,4},{6,5},{7,6},{8,11},{9,8},{10,9... | collective-permute-start | bytes 3538952 | tf_op jit(solution)/shard_map/ppermute | solution.py:23
  133.8 298.7 %reduce-scatter.15.cloned.1.call-start = ((), (), s32[]{:S(2)}) async-start(), calls=%async_computation.14 | async-start | bytes 3538944 | tf_op jit(solution)/shard_map/reduce_scatter | solution.py:254
  262.8 4.7 copy-start.25
  273.6 4.7 copy-start.25
  285.0 13.2 %copy-start.48 = (f32[768]{0:T(1024)S(1)}, f32[768]{0:T(1024)}, u32[]{:S(2)}) copy-start(f32[768]{0:T(1024)} %get-tuple-element.337) | copy-start | bytes 9220
  296.2 5.2 copy-start.36
  296.2 5.2 copy-start.38
  300.3 31.5 %copy-start.41 = (f32[2,128]{1,0:T(2,128)}, f32[2,128]{1,0:T(2,128)S(1)}, u32[]{:S(2)}) copy-start(f32[2,128]{1,0:T(2,128)S(1)} %broadcast_multiply_fusion.5) | copy-start | bytes 3076
  301.4 6.2 copy-start.50
  301.4 6.1 copy-start.6
  301.5 6.1 copy-start.60
  307.5 4.7 copy-start.15
  307.6 5.6 copy-start.28
  307.6 5.6 copy-start.39
  307.6 5.6 copy-start.46
  318.8 10.6 %slice-start = ((s8[4718592]{0:T(1024)(128)(4,1)}), s8[4194304]{0:T(1024)(128)(4,1)S(1)}, s32[]{:S(2)}) async-start(s8[4718592]{0:T(1024)(128)(4,1)} %bitcast.249), calls=%async_computation.22 | async-start | bytes 8388608
  321.2 8.2 copy-start.19
  321.2 8.2 copy-start.7
  321.2 8.2 copy-start.51
  321.2 8.2 slice-start.1
  331.8 6.9 copy-start.34
  338.9 4.3 copy-start.22
  338.9 4.3 copy-start.43
  338.9 4.3 copy-start.49
  340.5 5.3 copy-start.2
  357.1 5.3 copy-start.2
  386.1 95.9 %reduce-scatter.13.cloned.1.call-start = ((), (), s32[]{:S(2)}) async-start(), calls=%async_computation.13 | async-start | bytes 3538944 | tf_op jit(solution)/shard_map/reduce_scatter | solution.py:251
  400.2 155.0 %reduce-scatter.25.cloned.1.call-start = ((), (), s32[]{:S(2)}) async-start(), calls=%async_computation.19 | async-start | bytes 4423680
  488.6 99.1 %reduce-scatter.17.cloned.1.call-start = ((), (), s32[]{:S(2)}) async-start(), calls=%async_computation.15 | async-start | bytes 1474560 | tf_op jit(solution)/shard_map/reduce_scatter | solution.py:284
  491.3 182.4 %reduce-scatter.19.cloned.1.call-start = ((), (), s32[]{:S(2)}) async-start(), calls=%async_computation.16 | async-start | bytes 5898240 | tf_op jit(solution)/shard_map/reduce_scatter | solution.py:287
  495.8 266.0 %reduce-scatter.21.cloned.1.call-start = ((), (), s32[]{:S(2)}) async-start(), calls=%async_computation.17 | async-start | bytes 5898240 | tf_op jit(solution)/shard_map/reduce_scatter | solution.py:293
  501.2 283.5 %reduce-scatter.27.cloned.1.call-start = ((), (), s32[]{:S(2)}) async-start(), calls=%async_computation.20 | async-start | bytes 245760
  503.1 302.3 %reduce-scatter.23.cloned.1.call-start = ((), (), s32[]{:S(2)}) async-start(), calls=%async_computation.18 | async-start | bytes 245760 | tf_op jit(solution)/shard_map/reduce_scatter | solution.py:296
  505.3 256.6 %copy-start.67 = (u32[32]{0:T(128)S(1)}, u32[32]{0:T(128)}, u32[]{:S(2)}) copy-start(u32[32]{0:T(128)} %constant.123) | copy-start | bytes 388
  505.3 258.6 %copy-start.57 = (bf16[3072]{0:T(1024)(128)(2,1)S(1)}, bf16[3072]{0:T(1024)(128)(2,1)}, u32[]{:S(2)}) copy-start(bf16[3072]{0:T(1024)(128)(2,1)} %get-tuple-element.415) | copy-start | bytes 18436
  505.3 269.9 %copy-start.33 = (bf16[2,128,768]{2,1,0:T(8,128)(2,1)S(1)}, bf16[2,128,768]{2,1,0:T(8,128)(2,1)}, u32[]{:S(2)}) copy-start(bf16[2,128,768]{2,1,0:T(8,128)(2,1)} %copy.89) | copy-start | bytes 1179652
  505.3 269.9 %copy-start.66 = (bf16[2,128,768]{2,1,0:T(8,128)(2,1)S(1)}, bf16[2,128,768]{2,1,0:T(8,128)(2,1)}, u32[]{:S(2)}) copy-start(bf16[2,128,768]{2,1,0:T(8,128)(2,1)} %reduce-scatter.13.cloned.1.call-done) | copy-start | bytes 1179652
  505.3 380.5 %all-reduce.5.cloned.1.call-start = ((), (), s32[]{:S(2)}) async-start(), calls=%async_computation.21 | async-start | bytes 7667712 | tf_op jit(solution)/shard_map/psum | solution.py:304
  885.9 4.7 copy-start.27
  (50 other events, 111.5 us)
Sparse Core Ops, SparseCore 0:
  9.6 72.6 all-gather.7
  86.4 30.7 all-gather.11
  119.7 32.2 all-gather.9
  153.4 41.7 all-gather.13
  196.6 95.0 all-gather.15
  386.2 46.2 reduce-scatter.14
  435.9 46.0 reduce-scatter.12
  488.7 66.4 reduce-scatter.24
  558.1 29.4 reduce-scatter.16
  589.8 83.8 reduce-scatter.18
  676.0 85.7 reduce-scatter.20
  764.5 20.1 reduce-scatter.26
  787.5 17.7 reduce-scatter.22
  809.5 76.2 all-reduce.4
